TPU v7x, 128 devices: a whole 4x4x4 slice. The times are simulated.
128 devices in a mesh: row: 16 (over y, z_hi, core), col: 8 (over z_lo, x).
Axes of the slice: x: 4, y: 4, z: 4 (z_hi: 2, z_lo: 2; z = z_hi * 2 + z_lo), core: 2. Of those that a mesh axis runs over, the one named last changes fastest.
Arguments:
- features: bfloat16 [65536, 256], P('row', 'col'), may hold values from -12 to 12
- tile_vals: bfloat16 [4096, 1024, 128], P('row', 'col'), may hold values from 0 to 4, as said below
- tile_src: int32 [16, 2048], P('row', 'col'), may hold values from 0 to 31
- row_counts: int32 [16, 512], P('row', 'col'), may hold values from 1 to 6, as said below
Outputs:
- propagated: bfloat16 [65536, 256], P(('row', 'col'))
Inputs may be any that keep to these rules, and one draw needn't show every extreme that they name: `tile_vals`: each entry is zero or a weight between 0.25 and 4. `row_counts`: on every group the 64 counts sum to at most 256; some groups reach 256 exactly.
All inputs are finite; a program needn't handle non-finite values.
Results may differ from a plain program's by a relative error of at most 0.009.
Values may be sent and summed in bfloat16 or wider, within the bound.
A program may use at most 128 MiB of HBM per device.

v0:
```python
import jax
import jax.numpy as jnp
from jax import lax
from jax.sharding import PartitionSpec as P

ITERS = 3


TELEPORT = 0.1


def slot_block():
    return 64


def slot_layout(counts, tile_max):
    row_ends = jnp.cumsum(counts, dtype=jnp.int32)
    slot_ids = jnp.arange(tile_max, dtype=jnp.int32)
    dest_tiles = jnp.sum(
        (row_ends[None, :] <= slot_ids[:, None]).astype(jnp.int32), axis=1, dtype=jnp.int32
    )
    live_slots = slot_ids < row_ends[-1]
    return (dest_tiles, live_slots, row_ends)


def tile_products(
    tile_vals, sources, dest_tiles, live_slots, source_rows, turn_count, dest_count, block_slots
):
    tile_size = tile_vals.shape[1]
    feat_width = source_rows.shape[1]
    grouped = source_rows.reshape(-1, tile_size, feat_width)

    def one_turn(turn_index, running):
        first_slot = (turn_index * block_slots).astype(jnp.int32)
        tile_block = lax.dynamic_slice_in_dim(tile_vals, first_slot, block_slots, 0)
        picked = jnp.take(
            grouped, lax.dynamic_slice_in_dim(sources, first_slot, block_slots, 0), axis=0
        )
        products = jnp.einsum(
            "tsd,tsf->tdf", tile_block, picked, preferred_element_type=jnp.float32
        )
        keep_mask = lax.dynamic_slice_in_dim(live_slots, first_slot, block_slots, 0)
        products = jnp.where(keep_mask[:, None, None], products, 0.0)
        targets = lax.dynamic_slice_in_dim(dest_tiles, first_slot, block_slots, 0)
        return running.at[targets].add(products, mode="drop")

    running = jnp.zeros((dest_count, tile_size, feat_width), jnp.float32)
    running = lax.fori_loop(0, turn_count, one_turn, running)
    return running.reshape(dest_count * tile_size, feat_width)


def on_device(features, tile_vals, tile_src, row_counts):
    tile_max = tile_vals.shape[0]
    tile_size = tile_vals.shape[1]
    dest_count = row_counts.shape[1]
    block_slots = slot_block()
    dest_tiles, live_slots, row_ends = slot_layout(row_counts[0], tile_max)
    sources = tile_src[0]
    own_rows = lax.all_to_all(features, "col", split_axis=0, concat_axis=1, tiled=True)
    source_rows = lax.all_gather(own_rows, "col", axis=0, tiled=True)
    unit_vector = jnp.ones((tile_size,), jnp.bfloat16)
    column_sums = jnp.einsum(
        "tsd,s->td", tile_vals, unit_vector, preferred_element_type=jnp.float32
    )
    column_sums = jnp.where(live_slots[:, None], column_sums, 0.0)
    weight_sums = (
        jnp.zeros((dest_count, tile_size), jnp.float32).at[dest_tiles].add(column_sums, mode="drop")
    )
    degree = 1.0 + lax.psum_scatter(
        weight_sums.reshape(-1).astype(jnp.bfloat16), "row", scatter_dimension=0, tiled=True
    ).astype(jnp.float32)
    turn_count = tile_max // block_slots
    restart = TELEPORT * own_rows.astype(jnp.float32)
    iterate = own_rows
    for iteration in range(ITERS):
        if iteration > 0:
            source_rows = lax.all_gather(iterate, "col", axis=0, tiled=True)
        term_rows = tile_products(
            tile_vals,
            sources,
            dest_tiles,
            live_slots,
            source_rows,
            turn_count,
            dest_count,
            block_slots,
        )
        summed = lax.psum_scatter(
            term_rows.astype(jnp.bfloat16), "row", scatter_dimension=0, tiled=True
        ).astype(jnp.float32)
        iterate = (
            (1.0 - TELEPORT) * (summed + iterate.astype(jnp.float32)) / degree[:, None] + restart
        ).astype(jnp.bfloat16)
    return iterate


def solution(mesh):
    placed = (P("row", "col"), P("row", "col", None), P("row", "col"), P("row", "col"))
    return jax.shard_map(
        on_device, mesh=mesh, in_specs=placed, out_specs=P(("row", "col"), None), check_vma=False
    )
```

profile of v0, /device:TPU:0, one launch (start us, length us, event | category | flops | bytes accessed | tf_op | source)
XLA Modules:
  0.0 794.9 jit_solution(8272259294167142320)
XLA Ops:
  7.5 13.0 %all_to_all.19 = bf16[8,512,32]{1,2,0:T(8,128)(2,1)} all-to-all(bf16[8,512,32]{1,2,0:T(8,128)(2,1)S(1)} %bitcast.37), channel_id=1, replica_groups=mesh['row'=16,'col'=8] {'col'}, dimensions={0} | all-to-all | bytes 524288 | tf_op jit(solution)/shard_map/all_to_all | solution.py:59
  22.1 11.9 %copy.53 = bf16[256,128,128]{1,2,0:T(8,128)(2,1)} copy(bf16[256,128,128]{2,1,0:T(8,128)(2,1)} %param.13) | data formatting | bytes 16777216 | tf_op jit(solution)/shard_map/while | solution.py:48
  34.8 27.1 %all-gather.4.cloned.1.call-done = bf16[4096,256]{0,1:T(8,128)(2,1)} async-done(((bf16[512,256]{0,1:T(8,128)(2,1)}), bf16[4096,256]{0,1:T(8,128)(2,1)}) %all-gather.4.cloned.1.call-update) | async-done | bytes 2097168 | tf_op jit(solution)/shard_map/all_gather | solution.py:60
  61.9 3.3 copy.58
  65.2 4.2 broadcast.73.clone.1
  69.4 113.3 %while.39 = (s32[]{:T(128)}, f32[64,128,256]{2,1,0:T(8,128)}, s32[256]{0:T(256)S(1)}, pred[256]{0:T(512)(128)(4,1)S(1)}, bf16[256,128,128]{1,2,0:T(8,128)(2,1)},...) while((s32[]{:T(128)}, f32[64,128,256]{2,1,0:T(8,128)}, ...), condition=%wide.region_4.6_spmd, body=%wide.region_2.5_spmd.sunk | while | flops 543163968 | bytes 48240872 | solution.py:48
  69.5 2.8 gather_fusion
  72.4 7.4 broadcast_select_fusion.6
  79.8 18.4 %scatter_fusion = f32[64,128,256]{2,1,0:T(8,128)} fusion(f32[64,128,256]{2,1,0:T(8,128)} %get-tuple-element.687, s32[64]{0:T(128)S(1)} %compare_select_fusion.13, f32[64,128,256]{2,1,0:T(8,128)} %broadcast_select_fusion.6), kind=kCustom, calls=%fused_computation.3.clone.1 | custom fusion | flops 2097152 | bytes 25166080 | tf_op jit(solution)/shard_map/while/body/eval_jaxpr/scatter-add | solution.py:45
  98.3 2.8 gather_fusion
  101.2 7.4 broadcast_select_fusion.6
  108.6 18.6 %scatter_fusion = f32[64,128,256]{2,1,0:T(8,128)} fusion(f32[64,128,256]{2,1,0:T(8,128)} %get-tuple-element.687, s32[64]{0:T(128)S(1)} %compare_select_fusion.13, f32[64,128,256]{2,1,0:T(8,128)} %broadcast_select_fusion.6), kind=kCustom, calls=%fused_computation.3.clone.1 | custom fusion | flops 2097152 | bytes 25166080 | tf_op jit(solution)/shard_map/while/body/eval_jaxpr/scatter-add | solution.py:45
  127.3 2.8 gather_fusion
  130.1 7.4 broadcast_select_fusion.6
  137.6 17.4 %scatter_fusion = f32[64,128,256]{2,1,0:T(8,128)} fusion(f32[64,128,256]{2,1,0:T(8,128)} %get-tuple-element.687, s32[64]{0:T(128)S(1)} %compare_select_fusion.13, f32[64,128,256]{2,1,0:T(8,128)} %broadcast_select_fusion.6), kind=kCustom, calls=%fused_computation.3.clone.1 | custom fusion | flops 2097152 | bytes 25166080 | tf_op jit(solution)/shard_map/while/body/eval_jaxpr/scatter-add | solution.py:45
  155.1 2.8 gather_fusion
  158.0 7.4 broadcast_select_fusion.6
  165.4 17.4 %scatter_fusion = f32[64,128,256]{2,1,0:T(8,128)} fusion(f32[64,128,256]{2,1,0:T(8,128)} %get-tuple-element.687, s32[64]{0:T(128)S(1)} %compare_select_fusion.13, f32[64,128,256]{2,1,0:T(8,128)} %broadcast_select_fusion.6), kind=kCustom, calls=%fused_computation.3.clone.1 | custom fusion | flops 2097152 | bytes 25166080 | tf_op jit(solution)/shard_map/while/body/eval_jaxpr/scatter-add | solution.py:45
  182.8 6.0 convert_element_type.59
  188.8 6.4 copy.59
  197.1 4.6 fusion.40
  201.7 1.7 scatter_custom_fusion.3
  203.4 65.6 %all-reduce = bf16[8192]{0:T(1024)(128)(2,1)S(1)} all-reduce(bf16[8192]{0:T(1024)(128)(2,1)S(1)} %convert_bitcast_fusion), channel_id=3, replica_groups=mesh['row'=16,'col'=8] {'row'}, use_global_device_ids=true, to_apply=%region_7.9.clone | all-reduce | flops 8192 | bytes 32768
  269.0 6.6 reduce-scatter.4.cloned.1.call-done
  275.6 1.8 fusion.30
  277.6 39.8 %all-gather.6.cloned.1.call-done = bf16[4096,256]{0,1:T(8,128)(2,1)} async-done(((bf16[512,256]{0,1:T(8,128)(2,1)}), bf16[4096,256]{0,1:T(8,128)(2,1)}) %all-gather.6.cloned.1.call-update) | async-done | bytes 2097168 | tf_op jit(solution)/shard_map/all_gather | solution.py:77
  317.4 3.3 copy.60
  320.7 4.2 broadcast.73.clone
  324.9 113.3 %while.40 = (s32[]{:T(128)}, f32[64,128,256]{2,1,0:T(8,128)}, s32[256]{0:T(256)S(1)}, pred[256]{0:T(512)(128)(4,1)S(1)}, bf16[256,128,128]{1,2,0:T(8,128)(2,1)},...) while((s32[]{:T(128)}, f32[64,128,256]{2,1,0:T(8,128)}, ...), condition=%wide.region_10.12_spmd, body=%wide.region_8.11_spmd.sunk | while | flops 543163968 | bytes 48240872 | solution.py:48
  325.0 2.8 gather_fusion.1
  327.9 7.4 broadcast_select_fusion.7
  335.3 18.4 %scatter_fusion.1 = f32[64,128,256]{2,1,0:T(8,128)} fusion(f32[64,128,256]{2,1,0:T(8,128)} %get-tuple-element.720, s32[64]{0:T(128)S(1)} %compare_select_fusion.14, f32[64,128,256]{2,1,0:T(8,128)} %broadcast_select_fusion.7), kind=kCustom, calls=%fused_computation.4.clone.1 | custom fusion | flops 2097152 | bytes 25166080 | tf_op jit(solution)/shard_map/while/body/eval_jaxpr/scatter-add | solution.py:45
  353.8 2.8 gather_fusion.1
  356.7 7.4 broadcast_select_fusion.7
  364.1 18.6 %scatter_fusion.1 = f32[64,128,256]{2,1,0:T(8,128)} fusion(f32[64,128,256]{2,1,0:T(8,128)} %get-tuple-element.720, s32[64]{0:T(128)S(1)} %compare_select_fusion.14, f32[64,128,256]{2,1,0:T(8,128)} %broadcast_select_fusion.7), kind=kCustom, calls=%fused_computation.4.clone.1 | custom fusion | flops 2097152 | bytes 25166080 | tf_op jit(solution)/shard_map/while/body/eval_jaxpr/scatter-add | solution.py:45
  382.8 2.8 gather_fusion.1
  385.6 7.4 broadcast_select_fusion.7
  393.1 17.4 %scatter_fusion.1 = f32[64,128,256]{2,1,0:T(8,128)} fusion(f32[64,128,256]{2,1,0:T(8,128)} %get-tuple-element.720, s32[64]{0:T(128)S(1)} %compare_select_fusion.14, f32[64,128,256]{2,1,0:T(8,128)} %broadcast_select_fusion.7), kind=kCustom, calls=%fused_computation.4.clone.1 | custom fusion | flops 2097152 | bytes 25166080 | tf_op jit(solution)/shard_map/while/body/eval_jaxpr/scatter-add | solution.py:45
  410.6 2.8 gather_fusion.1
  413.4 7.4 broadcast_select_fusion.7
  420.9 17.4 %scatter_fusion.1 = f32[64,128,256]{2,1,0:T(8,128)} fusion(f32[64,128,256]{2,1,0:T(8,128)} %get-tuple-element.720, s32[64]{0:T(128)S(1)} %compare_select_fusion.14, f32[64,128,256]{2,1,0:T(8,128)} %broadcast_select_fusion.7), kind=kCustom, calls=%fused_computation.4.clone.1 | custom fusion | flops 2097152 | bytes 25166080 | tf_op jit(solution)/shard_map/while/body/eval_jaxpr/scatter-add | solution.py:45
  438.3 6.0 convert_element_type.67
  444.3 6.4 copy.61
  450.7 80.1 %reduce-scatter.6.cloned.1.call-done = bf16[512,256]{0,1:T(8,128)(2,1)} async-done(((bf16[8192,256]{0,1:T(8,128)(2,1)}), bf16[512,256]{0,1:T(8,128)(2,1)}) %reduce-scatter.6.cloned.1.call-update) | async-done | bytes 262160 | tf_op jit(solution)/shard_map/reduce_scatter | solution.py:88
  530.8 1.9 fusion.31
  532.8 39.9 %all-gather.8.cloned.1.call-done = bf16[4096,256]{0,1:T(8,128)(2,1)} async-done(((bf16[512,256]{0,1:T(8,128)(2,1)}), bf16[4096,256]{0,1:T(8,128)(2,1)}) %all-gather.8.cloned.1.call-update) | async-done | bytes 2097168 | tf_op jit(solution)/shard_map/all_gather | solution.py:77
  572.7 3.3 copy.62
  576.0 4.2 broadcast.73
  580.3 113.3 %while.41 = (s32[]{:T(128)}, f32[64,128,256]{2,1,0:T(8,128)}, s32[256]{0:T(256)S(1)}, pred[256]{0:T(512)(128)(4,1)S(1)}, bf16[256,128,128]{1,2,0:T(8,128)(2,1)},...) while((s32[]{:T(128)}, f32[64,128,256]{2,1,0:T(8,128)}, ...), condition=%wide.region_14.16_spmd, body=%wide.region_12.15_spmd.sunk | while | flops 543163968 | bytes 48240872 | solution.py:48
  580.3 2.8 gather_fusion.2
  583.2 7.4 broadcast_select_fusion.8
  590.6 18.4 %scatter_fusion.2 = f32[64,128,256]{2,1,0:T(8,128)} fusion(f32[64,128,256]{2,1,0:T(8,128)} %get-tuple-element.753, s32[64]{0:T(128)S(1)} %compare_select_fusion.15, f32[64,128,256]{2,1,0:T(8,128)} %broadcast_select_fusion.8), kind=kCustom, calls=%fused_computation.5.clone.1 | custom fusion | flops 2097152 | bytes 25166080 | tf_op jit(solution)/shard_map/while/body/eval_jaxpr/scatter-add | solution.py:45
  609.1 2.8 gather_fusion.2
  612.0 7.4 broadcast_select_fusion.8
  619.4 18.6 %scatter_fusion.2 = f32[64,128,256]{2,1,0:T(8,128)} fusion(f32[64,128,256]{2,1,0:T(8,128)} %get-tuple-element.753, s32[64]{0:T(128)S(1)} %compare_select_fusion.15, f32[64,128,256]{2,1,0:T(8,128)} %broadcast_select_fusion.8), kind=kCustom, calls=%fused_computation.5.clone.1 | custom fusion | flops 2097152 | bytes 25166080 | tf_op jit(solution)/shard_map/while/body/eval_jaxpr/scatter-add | solution.py:45
  638.1 2.8 gather_fusion.2
  641.0 7.4 broadcast_select_fusion.8
  648.4 17.4 %scatter_fusion.2 = f32[64,128,256]{2,1,0:T(8,128)} fusion(f32[64,128,256]{2,1,0:T(8,128)} %get-tuple-element.753, s32[64]{0:T(128)S(1)} %compare_select_fusion.15, f32[64,128,256]{2,1,0:T(8,128)} %broadcast_select_fusion.8), kind=kCustom, calls=%fused_computation.5.clone.1 | custom fusion | flops 2097152 | bytes 25166080 | tf_op jit(solution)/shard_map/while/body/eval_jaxpr/scatter-add | solution.py:45
  665.9 2.8 gather_fusion.2
  668.8 7.4 broadcast_select_fusion.8
  676.2 17.4 %scatter_fusion.2 = f32[64,128,256]{2,1,0:T(8,128)} fusion(f32[64,128,256]{2,1,0:T(8,128)} %get-tuple-element.753, s32[64]{0:T(128)S(1)} %compare_select_fusion.15, f32[64,128,256]{2,1,0:T(8,128)} %broadcast_select_fusion.8), kind=kCustom, calls=%fused_computation.5.clone.1 | custom fusion | flops 2097152 | bytes 25166080 | tf_op jit(solution)/shard_map/while/body/eval_jaxpr/scatter-add | solution.py:45
  693.6 5.9 convert_element_type.72
  699.5 6.4 copy.63
  705.9 80.2 %reduce-scatter.8.cloned.1.call-done = bf16[512,256]{0,1:T(8,128)(2,1)} async-done(((bf16[8192,256]{0,1:T(8,128)(2,1)}), bf16[512,256]{0,1:T(8,128)(2,1)}) %reduce-scatter.8.cloned.1.call-update) | async-done | bytes 262160 | tf_op jit(solution)/shard_map/reduce_scatter | solution.py:88
  (83 shorter events, 9.8 us)
Async XLA Ops:
  6.5 55.4 %all-gather.4.cloned.1.call-start = ((), (), s32[]{:S(2)}) async-start(), calls=%async_computation.4 | async-start | bytes 2359296 | tf_op jit(solution)/shard_map/all_gather | solution.py:60
  20.5 255.1 %reduce-scatter.4.cloned.1.call-start = ((), (), s32[]{:S(2)}) async-start(), calls=%async_computation.5 | async-start | bytes 4456448 | tf_op jit(solution)/shard_map/reduce_scatter | solution.py:88
  65.2 4.3 copy-start.3
  195.1 0.7 copy-start.4
  195.2 122.2 %all-gather.6.cloned.1.call-start = ((), (), s32[]{:S(2)}) async-start(), calls=%async_computation.6 | async-start | bytes 2359296 | tf_op jit(solution)/shard_map/all_gather | solution.py:77
  197.0 78.6 %copy-start = (bf16[8,512,32]{1,2,0:T(8,128)(2,1)S(1)}, bf16[8,512,32]{1,2,0:T(8,128)(2,1)}, u32[]{:S(2)}) copy-start(bf16[8,512,32]{1,2,0:T(8,128)(2,1)} %all_to_all.19) | copy-start | bytes 786436
  277.4 253.4 %reduce-scatter.6.cloned.1.call-start = ((), (), s32[]{:S(2)}) async-start(), calls=%async_computation.7 | async-start | bytes 4456448 | tf_op jit(solution)/shard_map/reduce_scatter | solution.py:88
  450.6 80.2 %copy-start.2 = (bf16[512,256]{0,1:T(8,128)(2,1)S(1)}, bf16[512,256]{0,1:T(8,128)(2,1)}, u32[]{:S(2)}) copy-start(bf16[512,256]{0,1:T(8,128)(2,1)} %reduce-scatter.4.cloned.1.call-done) | copy-start | bytes 786436
  450.6 122.1 %all-gather.8.cloned.1.call-start = ((), (), s32[]{:S(2)}) async-start(), calls=%async_computation.8 | async-start | bytes 2359296 | tf_op jit(solution)/shard_map/all_gather | solution.py:77
  532.7 253.4 %reduce-scatter.8.cloned.1.call-start = ((), (), s32[]{:S(2)}) async-start(), calls=%async_computation.9 | async-start | bytes 4456448 | tf_op jit(solution)/shard_map/reduce_scatter | solution.py:88
  705.9 80.2 %copy-start.1 = (bf16[512,256]{0,1:T(8,128)(2,1)S(1)}, bf16[512,256]{0,1:T(8,128)(2,1)}, u32[]{:S(2)}) copy-start(bf16[512,256]{0,1:T(8,128)(2,1)} %fusion.31) | copy-start | bytes 786436
Sparse Core Ops, SparseCore 0:
  20.6 41.2 all-gather.3
  195.3 80.2 reduce-scatter.3
  277.5 39.8 all-gather.5
  450.8 80.0 reduce-scatter.5
  532.8 39.8 all-gather.7
  706.1 80.0 reduce-scatter.7
where the time goes:
time: 796 us; the launch traced here: 795 us
  waiting for transfers between devices  274 us (34%)
  other arithmetic  243 us (31%)
  matrix products  92.9 us (12%)
  local copies, waits for them, and re-layouts  92.3 us (12%)
  blocking collectives  78.6 us (10%)
  between operations  14.2 us (2%)
    scatter-add x12, other arithmetic, one_turn(): return running.at[targets].add(products, mode='drop')  215 us
    reduce_scatter x3, waiting for transfers between devices, on_device(): lax.psum_scatter(term_rows.astype(jnp.bfloat16), 'row', scatter_dimension...  167 us
    dot_general x12, matrix products, one_turn(): jnp.einsum('tsd,tsf->tdf', tile_block, picked, preferred_element_type=jnp...  88.3 us
    all_gather x2, waiting for transfers between devices, on_device(): source_rows = lax.all_gather(iterate, 'col', axis=0, tiled=True)  79.7 us
    unnamed x1, blocking collectives  65.6 us
    gather x12, local copies, waits for them, and re-layouts, one_turn(): jnp.take(grouped, lax.dynamic_slice_in_dim(sources, first_slot, block_slo...  33.5 us
    all_gather x1, waiting for transfers between devices, on_device(): source_rows = lax.all_gather(own_rows, 'col', axis=0, tiled=True)  27.1 us
    while x4, local copies, waits for them, and re-layouts, tile_products(): running = lax.fori_loop(0, turn_count, one_turn, running)  21.7 us
  transfers between devices with their start and end apart: 6, of which 6 were waited for; matrix products, arithmetic and copies ran while one was open for 3% of the time, Pallas kernels for 0%

commit v1 on v0

v1 whole, which is shorter than its diff:
```python
import functools

import jax
import jax.numpy as jnp
from jax import lax
from jax.experimental import pallas as pl
from jax.experimental.pallas import tpu as pltpu
from jax.sharding import PartitionSpec as P

ITERS = 3
TELEPORT = 0.1
TILE = 128
SLOTS = 256
DESTS = 64
SRCS = 32
MOST = 6
FEATS = 256
CHUNKS = 2
WIDE = FEATS // CHUNKS
GROUP = 32 // CHUNKS
TAIL = 16
MESH = pl.DeviceIdType.MESH
F32, BF16 = jnp.float32, jnp.bfloat16


def rows_of(step, chunk):
    return WIDE + (TAIL if (step, chunk) == (0, 0) else 0)


def scratch_layout():
    shapes = {"w": pltpu.VMEM((SLOTS, TILE, TILE), BF16)}
    for k in range(ITERS):
        for ch in range(CHUNKS):
            m = rows_of(k, ch)
            tag = (k, ch)
            shapes["x", tag] = pltpu.VMEM((SRCS + 1, m, TILE), BF16)
            shapes["give", tag] = pltpu.VMEM((8, 4, m, TILE), BF16)
            shapes["take", tag] = pltpu.VMEM((8, 4, m, TILE), BF16)
            shapes["own", tag] = pltpu.VMEM((8, 4, m, TILE), BF16)
            shapes["far_p", tag] = pltpu.VMEM((2, 2, m, TILE), BF16)
            shapes["far_m", tag] = pltpu.VMEM((2, 2, m, TILE), BF16)
            shapes["near_p", tag] = pltpu.VMEM((2, 4, m, TILE), BF16)
            shapes["near_m", tag] = pltpu.VMEM((2, 4, m, TILE), BF16)
            shapes["z_out", tag] = pltpu.VMEM((4, m, TILE), BF16)
            shapes["z_in", tag] = pltpu.VMEM((4, m, TILE), BF16)
            for kind, count in (("core", 8), ("far", 4), ("near", 8), ("z", 1), ("ag", 9)):
                shapes["s_" + kind, tag] = pltpu.SemaphoreType.DMA((count,))
                shapes["r_" + kind, tag] = pltpu.SemaphoreType.DMA((count,))
    shapes["w_sem"] = pltpu.SemaphoreType.DMA((1,))
    shapes["x_sem"] = pltpu.SemaphoreType.DMA((4,))
    shapes["scale"] = pltpu.VMEM((4, 1, TILE), F32)
    shapes["table"] = pltpu.SMEM((DESTS * MOST + DESTS,), jnp.int32)
    return shapes


def kernel(names, src, cnt, feats, w_hbm, out_ref, *scratch):
    ref = dict(zip(names, scratch))
    w, table, scale = ref["w"], ref["table"], ref["scale"]
    row, col = lax.axis_index("row"), lax.axis_index("col")
    core, zh, y = row % 2, (row // 2) % 2, row // 4
    x, zl = col % 4, col // 4
    other_core = (row + 1 - 2 * core, col)
    y_next = (((y + 1) % 4) * 4 + row % 4, col)
    y_prev = (((y + 3) % 4) * 4 + row % 4, col)
    z_far = (row + 2 - 4 * zh, col)
    z_near = (row, col + 4 - 8 * zl)
    x_next = (row, zl * 4 + (x + 1) % 4)
    x_prev = (row, zl * 4 + (x + 3) % 4)
    sends = []

    def remote(kind, tag, index, source, target, device, keep=True):
        copy = pltpu.make_async_remote_copy(
            src_ref=source,
            dst_ref=target,
            send_sem=ref["s_" + kind, tag].at[index],
            recv_sem=ref["r_" + kind, tag].at[index],
            device_id=device,
            device_id_type=MESH,
        )
        copy.start()
        if keep:
            sends.append(copy)

    def arrived(kind, tag, index, target):
        pltpu.make_async_remote_copy(
            src_ref=target,
            dst_ref=target,
            send_sem=ref["s_" + kind, tag].at[index],
            recv_sem=ref["r_" + kind, tag].at[index],
            device_id=other_core,
            device_id_type=MESH,
        ).wait_recv()

    barrier = pltpu.get_barrier_semaphore()
    peers = (other_core, y_next, y_prev, z_far, z_near, x_next, x_prev)
    for peer in peers:
        pl.semaphore_signal(barrier, inc=1, device_id=peer, device_id_type=MESH)
    w_copy = pltpu.make_async_copy(w_hbm, w, ref["w_sem"].at[0])
    loads = []
    for g in range(4):
        ch, part = g // (4 // CHUNKS), g % (4 // CHUNKS)
        first = pl.multiple_of(col * GROUP + part * 8, 8)
        target = ref["x", (0, ch)].at[pl.ds(0, SRCS), pl.ds(first, 8), :]
        loads.append(pltpu.make_async_copy(feats.at[g], target, ref["x_sem"].at[g]))
        loads[-1].start()
    w_copy.start()
    for k in range(ITERS):
        for ch in range(CHUNKS):
            xs = ref["x", (k, ch)]
            xs[SRCS] = jnp.zeros((rows_of(k, ch), TILE), BF16)
    first_row = lax.broadcasted_iota(jnp.int32, (SRCS, TAIL, TILE), 1) == 0
    ref["x", (0, 0)][0:SRCS, WIDE : WIDE + TAIL, :] = jnp.where(first_row, 1.0, 0.0).astype(BF16)
    pl.semaphore_wait(barrier, len(peers))

    def block(k, ch, who, half=None):
        xs = ref["x", (k, ch)]
        if k == 0:
            feat = pl.ds(pl.multiple_of(who * GROUP, GROUP), GROUP)
            if half is None:
                return xs.at[pl.ds(0, SRCS), feat, :]
            return xs.at[pl.ds(half * (SRCS // 2), SRCS // 2), feat, :]
        if half is None:
            return xs.at[pl.ds(who * 4, 4)]
        return xs.at[pl.ds(who * 4 + half * 2, 2)]

    z_col = col + 4 - 8 * zl
    next_col, prev_col = zl * 4 + (x + 1) % 4, zl * 4 + (x + 3) % 4
    far_col = zl * 4 + (x + 2) % 4
    z_next, z_prev = next_col + 4 - 8 * zl, prev_col + 4 - 8 * zl
    z_across = far_col + 4 - 8 * zl

    def gather_0(k, ch):
        mine = block(k, ch, col)
        for index, device in ((0, z_near), (1, x_next), (2, x_prev)):
            remote("ag", (k, ch), index, mine, mine, device)

    def gather_1(k, ch):
        theirs = block(k, ch, z_col)
        arrived("ag", (k, ch), 0, theirs)
        remote("ag", (k, ch), 3, theirs, theirs, x_next)
        remote("ag", (k, ch), 4, theirs, theirs, x_prev)

    def pass_on(k, ch, base, prev_who, next_who):
        arrived("ag", (k, ch), base, block(k, ch, prev_who))
        half = block(k, ch, prev_who, 0)
        remote("ag", (k, ch), base + 4, half, half, x_next)
        arrived("ag", (k, ch), base + 1, block(k, ch, next_who))
        half = block(k, ch, next_who, 1)
        remote("ag", (k, ch), base + 5, half, half, x_prev)

    def gather_2(k, ch):
        pass_on(k, ch, 1, prev_col, next_col)

    def gather_3(k, ch):
        pass_on(k, ch, 3, z_prev, z_next)

    def gather_4(k, ch):
        arrived("ag", (k, ch), 5, block(k, ch, far_col, 0))
        arrived("ag", (k, ch), 6, block(k, ch, far_col, 1))
        arrived("ag", (k, ch), 7, block(k, ch, z_across, 0))
        arrived("ag", (k, ch), 8, block(k, ch, z_across, 1))

    def build_table():
        def one(q, start):
            count = cnt[0, q]
            for j in range(MOST):
                slot = jnp.minimum(start + j, SLOTS - 1)
                table[q * MOST + j] = jnp.where(j < count, src[0, slot], SRCS)
            table[DESTS * MOST + q] = start
            return start + count

        lax.fori_loop(0, DESTS, one, jnp.int32(0))

    def products(k, ch, q):
        xs = ref["x", (k, ch)]
        start = table[DESTS * MOST + q]
        left = jnp.concatenate([xs[table[q * MOST + j]] for j in range(MOST)], axis=1)
        right = jnp.concatenate(
            [w[jnp.minimum(start + j, SLOTS - 1)] for j in range(MOST)], axis=0
        )
        return jnp.dot(left, right, preferred_element_type=F32)

    def tail_sum(terms):
        total = None
        for term in terms:
            part = jnp.sum(term[WIDE:, :].astype(F32), axis=0, keepdims=True)
            total = part if total is None else total + part
        return total

    def add_up(terms):
        total = terms[0][:WIDE, :].astype(F32)
        for term in terms[1:]:
            total = total + term[:WIDE, :].astype(F32)
        return total

    def put(target, terms):
        target[0:WIDE, :] = add_up(terms).astype(BF16)
        if terms[0].shape[0] > WIDE:
            total = tail_sum(terms)
            high = total.astype(BF16).astype(F32)
            low = total - high
            which = lax.broadcasted_iota(jnp.int32, (TAIL, TILE), 0)
            split = jnp.where(which == 0, high, jnp.where(which == 1, low, 0.0))
            target[WIDE : WIDE + TAIL, :] = split.astype(BF16)

    def first_dest(i, side):
        yi = i // 2
        hop = (2 + 3 * yi + 3 * ((yi * (yi - 1)) // 2)) % 4
        z = (1 - zh + i % 2) % 2
        return (((y + hop) % 4) * 4 + z * 2 + side) * 4

    def make_given(k, ch):
        give, take = ref["give", (k, ch)], ref["take", (k, ch)]

        def one(i, carry):
            q = first_dest(i, 1 - core)
            for t in range(4):
                put(give.at[i, t], [products(k, ch, q + t)])
            remote("core", (k, ch), i, give.at[i], take.at[i], other_core, keep=False)
            return carry

        lax.fori_loop(0, 8, one, 0)

    def make_own(k, ch, low, high):
        own, take = ref["own", (k, ch)], ref["take", (k, ch)]

        def one(i, carry):
            q = first_dest(i, core)
            terms = [products(k, ch, q + t) for t in range(4)]
            arrived("core", (k, ch), i, take.at[i])
            for t in range(4):
                put(own.at[i, t], [terms[t], take[i, t]])
            return carry

        lax.fori_loop(low, high, one, 0)

    def own_blocks(k, ch):
        tag = (k, ch)
        own = ref["own", tag]
        make_own(k, ch, 0, 2)
        for zi in range(2):
            remote("far", tag, zi, own.at[zi, 0:2], ref["far_p", tag].at[zi], y_next)
            remote("far", tag, 2 + zi, own.at[zi, 2:4], ref["far_m", tag].at[zi], y_prev)
        make_own(k, ch, 2, 6)
        for zi in range(2):
            remote("near", tag, zi, own.at[2 + zi, 2:4], ref["near_p", tag].at[zi, 2:4], y_next)
            remote("near", tag, 2 + zi, own.at[4 + zi, 0:2], ref["near_m", tag].at[zi, 0:2], y_prev)
        make_own(k, ch, 6, 8)

    def relay(k, ch, zi):
        tag = (k, ch)
        own, far_p, far_m = ref["own", tag], ref["far_p", tag], ref["far_m", tag]
        arrived("far", tag, zi, far_p.at[zi])
        for t in range(2):
            put(own.at[2 + zi, t], [own[2 + zi, t], far_p[zi, t]])
        remote("near", tag, 4 + zi, own.at[2 + zi, 0:2], ref["near_p", tag].at[zi, 0:2], y_next)
        arrived("far", tag, 2 + zi, far_m.at[zi])
        for t in range(2):
            put(own.at[4 + zi, 2 + t], [own[4 + zi, 2 + t], far_m[zi, t]])
        remote("near", tag, 6 + zi, own.at[4 + zi, 2:4], ref["near_m", tag].at[zi, 2:4], y_prev)

    def y_done(k, ch, zi):
        tag = (k, ch)
        arrived("near", tag, zi, ref["near_p", tag].at[zi, 2:4])
        arrived("near", tag, 2 + zi, ref["near_m", tag].at[zi, 0:2])
        arrived("near", tag, 4 + zi, ref["near_p", tag].at[zi, 0:2])
        arrived("near", tag, 6 + zi, ref["near_m", tag].at[zi, 2:4])

    def z_send(k, ch):
        tag = (k, ch)
        y_done(k, ch, 0)
        own, z_out = ref["own", tag], ref["z_out", tag]
        for t in range(4):
            put(z_out.at[t], [own[6, t], ref["near_p", tag][0, t], ref["near_m", tag][0, t]])
        remote("z", tag, 0, z_out, ref["z_in", tag], z_far)

    def finish(k, ch):
        tag = (k, ch)
        y_done(k, ch, 1)
        own, z_in = ref["own", tag], ref["z_in", tag]
        arrived("z", tag, 0, z_in)
        for t in range(4):
            terms = [own[7, t], ref["near_p", tag][1, t], ref["near_m", tag][1, t], z_in[t]]
            if tag == (0, 0):
                scale[t] = (1.0 - TELEPORT) / (1.0 + tail_sum(terms))
            here = col * 4 + t
            old = ref["x", tag][here, 0:WIDE, :].astype(F32)
            start = ref["x", (0, ch)][here, 0:WIDE, :].astype(F32)
            new = ((add_up(terms) + old) * scale[t] + TELEPORT * start).astype(BF16)
            if k + 1 < ITERS:
                ref["x", (k + 1, ch)][here, 0:WIDE, :] = new
            else:
                for g in range(8):
                    low = g * 32 + ch * GROUP
                    out_ref[t, low : low + GROUP, :] = new[g * GROUP : (g + 1) * GROUP, :]
        if k + 1 < ITERS:
            gather_0(k + 1, ch)

    per = 4 // CHUNKS
    for copy in loads[:per]:
        copy.wait()
    gather_0(0, 0)
    build_table()
    gather_1(0, 0)
    gather_2(0, 0)
    gather_3(0, 0)
    for copy in loads[per:]:
        copy.wait()
    gather_0(0, 1)
    gather_4(0, 0)
    w_copy.wait()
    for k in range(ITERS):
        for ch in range(CHUNKS):
            nxt = (k, 1) if ch == 0 else (k + 1, 0)
            busy = nxt[0] < ITERS
            make_given(k, ch)
            if busy:
                gather_1(*nxt)
            own_blocks(k, ch)
            if busy:
                gather_2(*nxt)
            relay(k, ch, 0)
            relay(k, ch, 1)
            if busy:
                gather_3(*nxt)
            z_send(k, ch)
            if busy:
                gather_4(*nxt)
            finish(k, ch)
    for copy in sends:
        copy.wait_send()
    for k in range(ITERS):
        for ch in range(CHUNKS):
            give, take = ref["give", (k, ch)], ref["take", (k, ch)]
            for i in range(8):
                pltpu.make_async_remote_copy(
                    src_ref=give.at[i],
                    dst_ref=take.at[i],
                    send_sem=ref["s_core", (k, ch)].at[i],
                    recv_sem=ref["r_core", (k, ch)].at[i],
                    device_id=other_core,
                    device_id_type=MESH,
                ).wait_send()


def on_device(features, tile_vals, tile_src, row_counts):
    feats = features.T.reshape(4, 8, SRCS, TILE).transpose(0, 2, 1, 3)
    shapes = scratch_layout()
    out = pl.pallas_call(
        functools.partial(kernel, tuple(shapes)),
        out_shape=jax.ShapeDtypeStruct((4, FEATS, TILE), BF16),
        in_specs=[pl.BlockSpec(memory_space=pltpu.SMEM)] * 2
        + [pl.BlockSpec(memory_space=pl.ANY)] * 2,
        out_specs=pl.BlockSpec(memory_space=pltpu.VMEM),
        scratch_shapes=list(shapes.values()),
        compiler_params=pltpu.CompilerParams(
            collective_id=0, has_side_effects=True, vmem_limit_bytes=58 * 2**20
        ),
        name="propagate",
    )(tile_src, row_counts, feats, tile_vals)
    return out.transpose(0, 2, 1).reshape(4 * TILE, FEATS)


def solution(mesh):
    placed = (P("row", "col"), P("row", "col", None), P("row", "col"), P("row", "col"))
    return jax.shard_map(
        on_device, mesh=mesh, in_specs=placed, out_specs=P(("row", "col"), None), check_vma=False
    )
```

time: 796 us -> 141 us (0.18)
  waiting for transfers between devices: 274 us -> 0 us
  other arithmetic: 243 us -> 0 us
  Pallas kernels: 0 us -> 139 us
  matrix products: 92.9 us -> 0 us
  local copies, waits for them, and re-layouts: 92.3 us -> 1.79 us
  blocking collectives: 78.6 us -> 0 us
  between operations: 14.2 us -> 0.01 us
    scatter-add x13 -> x0, other arithmetic: 217 us -> none  [the longest x12 215 us: one_turn(): return running.at[targets].add(products, mode='drop')]
    reduce_scatter x3 -> x0, waiting for transfers between devices: 167 us -> none  [on_device(): lax.psum_scatter(term_rows.astype(jnp.bfloat16), 'row', scatter_dimension...]
    pallas_call x0 -> x1, Pallas kernels: none -> 139 us  [on_device(): pl.pallas_call(functools.partial(kernel, tuple(shapes)), out_shape=jax.Sh...]
    all_gather x3 -> x0, waiting for transfers between devices: 107 us -> none  [the longest x2 79.7 us: on_device(): source_rows = lax.all_gather(iterate, 'col', axis=0, tiled=True)]
    dot_general x13 -> x0, matrix products: 92.9 us -> none  [the longest x12 88.3 us: one_turn(): jnp.einsum('tsd,tsf->tdf', tile_block, picked, preferred_element_type=jnp...]
    unnamed x1 -> x0, blocking collectives: 65.6 us -> none
    gather x12 -> x0, local copies, waits for them, and re-layouts: 33.5 us -> none  [one_turn(): jnp.take(grouped, lax.dynamic_slice_in_dim(sources, first_slot, block_slo...]
    convert_element_type x7 -> x0, other arithmetic: 22.6 us -> none  [the longest x3 17.9 us: on_device(): term_rows.astype(jnp.bfloat16)]
  transfers between devices with their start and end apart: 6 -> 0, of which waited for: 6 -> 0; matrix products, arithmetic and copies ran while one was open for 3% -> 0% of each run, Pallas kernels for 0% -> 0%
where the time goes in v1:
time: 141 us; the launch traced here: 140 us
  Pallas kernels  139 us (99%)
  local copies, waits for them, and re-layouts  1.79 us (1%)
    pallas_call x1, Pallas kernels, on_device(): pl.pallas_call(functools.partial(kernel, tuple(shapes)), out_shape=jax.Sh...  139 us

profile of v1, /device:TPU:0, one launch (start us, length us, event | category | flops | bytes accessed | tf_op | source)
XLA Modules:
  0.0 140.3 jit_solution(11647468060234041073)
XLA Ops:
  0.0 138.5 %propagate.1 = bf16[4,256,128]{2,1,0:T(8,128)(2,1)} custom-call(s32[1,256]{1,0:T(1,128)} %src.1, s32[1,64]{1,0:T(1,128)} %cnt.1, bf16[4,32,8,128]{3,2,1,0:T(8,128)(2,1)} %bitcast.8, bf16[256,128,128]{2,1,0:T(8,128)(2,1)} %w_hbm.1), custom_call_target="tpu_custom_call" | custom-call | tf_op jit(solution)/shard_map/propagate/pallas_call | solution.py:349
  138.5 1.8 %copy.5 = bf16[4,128,256]{2,1,0:T(8,128)(2,1)} copy(bf16[4,128,256]{1,2,0:T(8,128)(2,1)} %bitcast.7) | data formatting | bytes 524288 | tf_op jit(solution)/shard_map/transpose | solution.py:361

commit v2 on v1

--- a/solution.py
+++ b/solution.py
@@ -15,7 +15,7 @@
 SRCS = 32
 MOST = 6
 FEATS = 256
-CHUNKS = 2
+CHUNKS = 4
 WIDE = FEATS // CHUNKS
 GROUP = 32 // CHUNKS
 TAIL = 16
@@ -53,6 +53,25 @@
     return shapes
 
 
+NAMES = (
+    "load",
+    "weights",
+    "gather_0",
+    "gather_1",
+    "gather_2",
+    "gather_3",
+    "gather_4",
+    "give",
+    "own_far",
+    "own_rest",
+    "relay_0",
+    "relay_1",
+    "z_send",
+    "finish",
+)
+ORDER = ((2, 0, 0), (2, 0, 1), (2, 0, 2), (4, 0, 0), (3, 0, 0), (3, 0, 1), (3, 0, 2), (5, 0, 0), (4, 0, 1), (5, 0, 1), (4, 0, 2), (2, 0, 3), (5, 0, 2), (1, 0, 0), (0, 0, 2), (0, 0, 1), (0, 0, 0), (0, 0, 3), (6, 0, 0), (7, 0, 0), (6, 0, 1), (3, 0, 3), (7, 0, 1), (8, 0, 0), (6, 0, 2), (7, 0, 2), (8, 0, 1), (5, 0, 3), (4, 0, 3), (9, 0, 0), (10, 0, 0), (9, 0, 1), (10, 0, 1), (8, 0, 2), (6, 0, 3), (7, 0, 3), (12, 0, 0), (11, 0, 0), (9, 0, 2), (12, 0, 1), (11, 0, 1), (8, 0, 3), (10, 0, 2), (9, 0, 3), (13, 0, 0), (2, 1, 0), (10, 0, 3), (13, 0, 1), (2, 1, 1), (11, 0, 2), (12, 0, 2), (3, 1, 0), (4, 1, 0), (12, 0, 3), (3, 1, 1), (4, 1, 1), (11, 0, 3), (5, 1, 0), (13, 0, 2), (2, 1, 2), (5, 1, 1), (13, 0, 3), (2, 1, 3), (6, 1, 0), (7, 1, 0), (3, 1, 2), (4, 1, 2), (6, 1, 1), (7, 1, 1), (8, 1, 0), (3, 1, 3), (9, 1, 0), (5, 1, 2), (4, 1, 3), (8, 1, 1), (9, 1, 1), (10, 1, 0), (5, 1, 3), (11, 1, 0), (6, 1, 2), (7, 1, 2), (10, 1, 1), (11, 1, 1), (6, 1, 3), (7, 1, 3), (12, 1, 0), (8, 1, 2), (12, 1, 1), (9, 1, 2), (8, 1, 3), (10, 1, 2), (9, 1, 3), (13, 1, 0), (2, 2, 0), (13, 1, 1), (10, 1, 3), (2, 2, 1), (12, 1, 2), (3, 2, 0), (11, 1, 3), (11, 1, 2), (12, 1, 3), (4, 2, 0), (3, 2, 1), (4, 2, 1), (5, 2, 0), (13, 1, 2), (2, 2, 2), (5, 2, 1), (13, 1, 3), (6, 2, 0), (2, 2, 3), (7, 2, 0), (3, 2, 2), (4, 2, 2), (6, 2, 1), (7, 2, 1), (3, 2, 3), (8, 2, 0), (9, 2, 0), (5, 2, 2), (4, 2, 3), (8, 2, 1), (9, 2, 1), (5, 2, 3), (10, 2, 0), (11, 2, 0), (6, 2, 2), (7, 2, 2), (10, 2, 1), (6, 2, 3), (7, 2, 3), (8, 2, 2), (9, 2, 2), (12, 2, 1), (8, 2, 3), (12, 2, 0), (10, 2, 2), (9, 2, 3), (10, 2, 3), (11, 2, 3), (11, 2, 2), (11, 2, 1), (12, 2, 2), (12, 2, 3), (13, 2, 1), (13, 2, 0), (13, 2, 2), (13, 2, 3))
+
+
 def kernel(names, src, cnt, feats, w_hbm, out_ref, *scratch):
     ref = dict(zip(names, scratch))
     w, table, scale = ref["w"], ref["table"], ref["scale"]
@@ -68,7 +87,7 @@
     x_prev = (row, zl * 4 + (x + 3) % 4)
     sends = []
 
-    def remote(kind, tag, index, source, target, device, keep=True):
+    def remote(kind, tag, index, source, target, device, keep=True, begin=True):
         copy = pltpu.make_async_remote_copy(
             src_ref=source,
             dst_ref=target,
@@ -77,7 +96,8 @@
             device_id=device,
             device_id_type=MESH,
         )
-        copy.start()
+        if begin:
+            copy.start()
         if keep:
             sends.append(copy)
 
@@ -110,6 +130,19 @@
             xs[SRCS] = jnp.zeros((rows_of(k, ch), TILE), BF16)
     first_row = lax.broadcasted_iota(jnp.int32, (SRCS, TAIL, TILE), 1) == 0
     ref["x", (0, 0)][0:SRCS, WIDE : WIDE + TAIL, :] = jnp.where(first_row, 1.0, 0.0).astype(BF16)
+
+    def build_table():
+        def one(q, start):
+            count = cnt[0, q]
+            for j in range(MOST):
+                slot = jnp.minimum(start + j, SLOTS - 1)
+                table[q * MOST + j] = jnp.where(j < count, src[0, slot], SRCS)
+            table[DESTS * MOST + q] = start
+            return start + count
+
+        lax.fori_loop(0, DESTS, one, jnp.int32(0))
+
+    build_table()
     pl.semaphore_wait(barrier, len(peers))
 
     def block(k, ch, who, half=None):
@@ -131,8 +164,9 @@
 
     def gather_0(k, ch):
         mine = block(k, ch, col)
+        source = mine if k else feats.at[ch]
         for index, device in ((0, z_near), (1, x_next), (2, x_prev)):
-            remote("ag", (k, ch), index, mine, mine, device)
+            remote("ag", (k, ch), index, source, mine, device)
 
     def gather_1(k, ch):
         theirs = block(k, ch, z_col)
@@ -140,36 +174,29 @@
         remote("ag", (k, ch), 3, theirs, theirs, x_next)
         remote("ag", (k, ch), 4, theirs, theirs, x_prev)
 
-    def pass_on(k, ch, base, prev_who, next_who):
-        arrived("ag", (k, ch), base, block(k, ch, prev_who))
-        half = block(k, ch, prev_who, 0)
+    def pass_p(k, ch, base, who):
+        arrived("ag", (k, ch), base, block(k, ch, who))
+        half = block(k, ch, who, 0)
         remote("ag", (k, ch), base + 4, half, half, x_next)
-        arrived("ag", (k, ch), base + 1, block(k, ch, next_who))
-        half = block(k, ch, next_who, 1)
+
+    def pass_m(k, ch, base, who):
+        arrived("ag", (k, ch), base + 1, block(k, ch, who))
+        half = block(k, ch, who, 1)
         remote("ag", (k, ch), base + 5, half, half, x_prev)
 
     def gather_2(k, ch):
-        pass_on(k, ch, 1, prev_col, next_col)
+        pass_p(k, ch, 1, prev_col)
+        pass_m(k, ch, 1, next_col)
 
     def gather_3(k, ch):
-        pass_on(k, ch, 3, z_prev, z_next)
+        pass_p(k, ch, 3, z_prev)
+        pass_m(k, ch, 3, z_next)
 
     def gather_4(k, ch):
         arrived("ag", (k, ch), 5, block(k, ch, far_col, 0))
         arrived("ag", (k, ch), 6, block(k, ch, far_col, 1))
         arrived("ag", (k, ch), 7, block(k, ch, z_across, 0))
         arrived("ag", (k, ch), 8, block(k, ch, z_across, 1))
-
-    def build_table():
-        def one(q, start):
-            count = cnt[0, q]
-            for j in range(MOST):
-                slot = jnp.minimum(start + j, SLOTS - 1)
-                table[q * MOST + j] = jnp.where(j < count, src[0, slot], SRCS)
-            table[DESTS * MOST + q] = start
-            return start + count
-
-        lax.fori_loop(0, DESTS, one, jnp.int32(0))
 
     def products(k, ch, q):
         xs = ref["x", (k, ch)]
@@ -203,49 +230,71 @@
             split = jnp.where(which == 0, high, jnp.where(which == 1, low, 0.0))
             target[WIDE : WIDE + TAIL, :] = split.astype(BF16)
 
-    def first_dest(i, side):
-        yi = i // 2
+    def first_dest(yi, zi, side):
         hop = (2 + 3 * yi + 3 * ((yi * (yi - 1)) // 2)) % 4
-        z = (1 - zh + i % 2) % 2
+        z = (1 - zh + zi) % 2
         return (((y + hop) % 4) * 4 + z * 2 + side) * 4
 
     def make_given(k, ch):
         give, take = ref["give", (k, ch)], ref["take", (k, ch)]
 
-        def one(i, carry):
-            q = first_dest(i, 1 - core)
-            for t in range(4):
-                put(give.at[i, t], [products(k, ch, q + t)])
-            remote("core", (k, ch), i, give.at[i], take.at[i], other_core, keep=False)
+        def one(yi, carry):
+            sums = [products(k, ch, first_dest(yi, zi, 1 - core) + t) for zi in range(2) for t in range(4)]
+            for zi in range(2):
+                i = yi * 2 + zi
+                for t in range(4):
+                    put(give.at[i, t], [sums[zi * 4 + t]])
+                remote("core", (k, ch), i, give.at[i], take.at[i], other_core, keep=False)
             return carry
 
-        lax.fori_loop(0, 8, one, 0)
-
-    def make_own(k, ch, low, high):
+        lax.fori_loop(0, 4, one, 0)
+
+    def make_own(k, ch, yi):
         own, take = ref["own", (k, ch)], ref["take", (k, ch)]
-
-        def one(i, carry):
-            q = first_dest(i, core)
-            terms = [products(k, ch, q + t) for t in range(4)]
+        sums = [products(k, ch, first_dest(yi, zi, core) + t) for zi in range(2) for t in range(4)]
+        for zi in range(2):
+            i = yi * 2 + zi
             arrived("core", (k, ch), i, take.at[i])
             for t in range(4):
-                put(own.at[i, t], [terms[t], take[i, t]])
-            return carry
-
-        lax.fori_loop(low, high, one, 0)
-
-    def own_blocks(k, ch):
+                put(own.at[i, t], [sums[zi * 4 + t], take[i, t]])
+
+    def own_far(k, ch):
         tag = (k, ch)
         own = ref["own", tag]
-        make_own(k, ch, 0, 2)
+        make_own(k, ch, 0)
         for zi in range(2):
             remote("far", tag, zi, own.at[zi, 0:2], ref["far_p", tag].at[zi], y_next)
             remote("far", tag, 2 + zi, own.at[zi, 2:4], ref["far_m", tag].at[zi], y_prev)
-        make_own(k, ch, 2, 6)
+
+    def near_p(k, ch, **how):
+        tag, own = (k, ch), ref["own", (k, ch)]
         for zi in range(2):
-            remote("near", tag, zi, own.at[2 + zi, 2:4], ref["near_p", tag].at[zi, 2:4], y_next)
-            remote("near", tag, 2 + zi, own.at[4 + zi, 0:2], ref["near_m", tag].at[zi, 0:2], y_prev)
-        make_own(k, ch, 6, 8)
+            target = ref["near_p", tag].at[zi, 2:4]
+            remote("near", tag, zi, own.at[2 + zi, 2:4], target, y_next, **how)
+
+    def near_m(k, ch, **how):
+        tag, own = (k, ch), ref["own", (k, ch)]
+        for zi in range(2):
+            target = ref["near_m", tag].at[zi, 0:2]
+            remote("near", tag, 2 + zi, own.at[4 + zi, 0:2], target, y_prev, **how)
+
+    def own_rest(k, ch):
+        def one(yi, carry):
+            make_own(k, ch, yi)
+
+            @pl.when(yi == 1)
+            def _():
+                near_p(k, ch, keep=False)
+
+            @pl.when(yi == 2)
+            def _():
+                near_m(k, ch, keep=False)
+
+            return carry
+
+        lax.fori_loop(1, 4, one, 0)
+        near_p(k, ch, begin=False)
+        near_m(k, ch, begin=False)
 
     def relay(k, ch, zi):
         tag = (k, ch)
@@ -265,6 +314,12 @@
         arrived("near", tag, 2 + zi, ref["near_m", tag].at[zi, 0:2])
         arrived("near", tag, 4 + zi, ref["near_p", tag].at[zi, 0:2])
         arrived("near", tag, 6 + zi, ref["near_m", tag].at[zi, 2:4])
+
+    def relay_0(k, ch):
+        relay(k, ch, 0)
+
+    def relay_1(k, ch):
+        relay(k, ch, 1)
 
     def z_send(k, ch):
         tag = (k, ch)
@@ -293,40 +348,30 @@
                 for g in range(8):
                     low = g * 32 + ch * GROUP
                     out_ref[t, low : low + GROUP, :] = new[g * GROUP : (g + 1) * GROUP, :]
-        if k + 1 < ITERS:
-            gather_0(k + 1, ch)
-
-    per = 4 // CHUNKS
-    for copy in loads[:per]:
-        copy.wait()
-    gather_0(0, 0)
-    build_table()
-    gather_1(0, 0)
-    gather_2(0, 0)
-    gather_3(0, 0)
-    for copy in loads[per:]:
-        copy.wait()
-    gather_0(0, 1)
-    gather_4(0, 0)
-    w_copy.wait()
-    for k in range(ITERS):
-        for ch in range(CHUNKS):
-            nxt = (k, 1) if ch == 0 else (k + 1, 0)
-            busy = nxt[0] < ITERS
-            make_given(k, ch)
-            if busy:
-                gather_1(*nxt)
-            own_blocks(k, ch)
-            if busy:
-                gather_2(*nxt)
-            relay(k, ch, 0)
-            relay(k, ch, 1)
-            if busy:
-                gather_3(*nxt)
-            z_send(k, ch)
-            if busy:
-                gather_4(*nxt)
-            finish(k, ch)
+    def load(k, ch):
+        loads[ch].wait()
+
+    def weights(k, ch):
+        w_copy.wait()
+
+    tasks = dict(
+        load=load,
+        weights=weights,
+        gather_0=gather_0,
+        gather_1=gather_1,
+        gather_2=gather_2,
+        gather_3=gather_3,
+        gather_4=gather_4,
+        give=make_given,
+        own_far=own_far,
+        own_rest=own_rest,
+        relay_0=relay_0,
+        relay_1=relay_1,
+        z_send=z_send,
+        finish=finish,
+    )
+    for number, k, ch in ORDER:
+        tasks[NAMES[number]](k, ch)
     for copy in sends:
         copy.wait_send()
     for k in range(ITERS):

time: 141 us -> 123 us (0.87)
  Pallas kernels: 139 us -> 122 us
    pallas_call x1, Pallas kernels: 139 us -> 122 us  [on_device(): pl.pallas_call(functools.partial(kernel, tuple(shapes)), out_shape=jax.Sh...]
where the time goes in v2:
time: 123 us
  Pallas kernels  122 us (99%)
  local copies, waits for them, and re-layouts  1.79 us (1%)
    pallas_call x1, Pallas kernels, on_device(): pl.pallas_call(functools.partial(kernel, tuple(shapes)), out_shape=jax.Sh...  122 us

profile of v2, /device:TPU:0, one launch (start us, length us, event | category | flops | bytes accessed | tf_op | source)
XLA Modules:
  0.0 123.4 jit_solution(8853701588979191906)
XLA Ops:
  0.0 121.6 %propagate.1 = bf16[4,256,128]{2,1,0:T(8,128)(2,1)} custom-call(s32[1,256]{1,0:T(1,128)} %src.1, s32[1,64]{1,0:T(1,128)} %cnt.1, bf16[4,32,8,128]{3,2,1,0:T(8,128)(2,1)} %bitcast.8, bf16[256,128,128]{2,1,0:T(8,128)(2,1)} %w_hbm.1), custom_call_target="tpu_custom_call" | custom-call | tf_op jit(solution)/shard_map/propagate/pallas_call | solution.py:394
  121.6 1.8 %copy.5 = bf16[4,128,256]{2,1,0:T(8,128)(2,1)} copy(bf16[4,128,256]{1,2,0:T(8,128)(2,1)} %bitcast.7) | data formatting | bytes 524288 | tf_op jit(solution)/shard_map/transpose | solution.py:406

commit v3 on v2

v3 whole, which is shorter than its diff:
```python
import functools

import jax
import jax.numpy as jnp
from jax import lax
from jax.experimental import pallas as pl
from jax.experimental.pallas import tpu as pltpu
from jax.sharding import PartitionSpec as P

ITERS = 3
TELEPORT = 0.1
TILE = 128
SLOTS = 256
DESTS = 64
SRCS = 32
MOST = 6
FEATS = 256
CHUNKS = 4
WIDE = FEATS // CHUNKS
GROUP = 32 // CHUNKS
TAIL = 16
MESH = pl.DeviceIdType.MESH
F32, BF16 = jnp.float32, jnp.bfloat16


def rows_of(step, chunk):
    return WIDE + (TAIL if (step, chunk) == (0, 0) else 0)


def scratch_layout():
    shapes = {"w": pltpu.VMEM((SLOTS, TILE, TILE), BF16)}
    for k in range(ITERS):
        for ch in range(CHUNKS):
            m = rows_of(k, ch)
            tag = (k, ch)
            shapes["x", tag] = pltpu.VMEM((SRCS + 1, m, TILE), BF16)
            shapes["give", tag] = pltpu.VMEM((8, 4, m, TILE), BF16)
            shapes["take", tag] = pltpu.VMEM((8, 4, m, TILE), BF16)
            shapes["own", tag] = pltpu.VMEM((8, 4, m, TILE), BF16)
            shapes["far", tag] = pltpu.VMEM((2, 4, m, TILE), BF16)
            shapes["near_p", tag] = pltpu.VMEM((2, 4, m, TILE), BF16)
            shapes["near_m", tag] = pltpu.VMEM((2, 4, m, TILE), BF16)
            shapes["z_out", tag] = pltpu.VMEM((4, m, TILE), BF16)
            shapes["z_in", tag] = pltpu.VMEM((4, m, TILE), BF16)
            for kind, count in (("core", 4), ("y", 6), ("z", 1), ("ag", 9)):
                shapes["s_" + kind, tag] = pltpu.SemaphoreType.DMA((count,))
                shapes["r_" + kind, tag] = pltpu.SemaphoreType.DMA((count,))
    shapes["w_sem"] = pltpu.SemaphoreType.DMA((1,))
    shapes["x_sem"] = pltpu.SemaphoreType.DMA((4,))
    shapes["scale"] = pltpu.VMEM((4, 1, TILE), F32)
    shapes["table"] = pltpu.SMEM((DESTS * MOST + DESTS,), jnp.int32)
    return shapes


NAMES = (
    "load",
    "weights",
    "gather_0",
    "gather_1",
    "gather_2",
    "gather_3",
    "gather_4",
    "give",
    "own_0",
    "own_1",
    "z_send",
    "finish",
    "drain",
)
ORDER = ((2, 0, 0), (2, 0, 1), (2, 0, 2), (3, 0, 0), (4, 0, 0), (3, 0, 2), (0, 0, 2), (1, 0, 0), (5, 0, 0), (4, 0, 2), (4, 0, 1), (5, 0, 2), (3, 0, 1), (2, 0, 3), (0, 0, 0), (6, 0, 0), (7, 0, 0), (6, 0, 2), (7, 0, 2), (8, 0, 0), (3, 0, 3), (9, 0, 0), (8, 0, 2), (9, 0, 2), (4, 0, 3), (5, 0, 1), (10, 0, 0), (5, 0, 3), (0, 0, 1), (0, 0, 3), (6, 0, 1), (7, 0, 1), (6, 0, 3), (11, 0, 0), (2, 1, 0), (10, 0, 2), (8, 0, 1), (7, 0, 3), (3, 1, 0), (9, 0, 1), (11, 0, 2), (2, 1, 2), (10, 0, 1), (8, 0, 3), (9, 0, 3), (6, 1, 0), (3, 1, 2), (7, 1, 0), (11, 0, 1), (2, 1, 1), (10, 0, 3), (8, 1, 0), (9, 1, 0), (6, 1, 2), (3, 1, 1), (7, 1, 2), (11, 0, 3), (2, 1, 3), (10, 1, 0), (8, 1, 2), (6, 1, 1), (7, 1, 1), (3, 1, 3), (9, 1, 2), (11, 1, 0), (2, 2, 0), (10, 1, 2), (8, 1, 1), (9, 1, 1), (6, 1, 3), (3, 2, 0), (7, 1, 3), (11, 1, 2), (10, 1, 1), (2, 2, 2), (8, 1, 3), (6, 2, 0), (7, 2, 0), (3, 2, 2), (11, 1, 1), (2, 2, 1), (9, 1, 3), (10, 1, 3), (8, 2, 0), (9, 2, 0), (3, 2, 1), (6, 2, 2), (7, 2, 2), (11, 1, 3), (2, 2, 3), (12, 1, 1), (8, 2, 2), (9, 2, 2), (6, 2, 1), (3, 2, 3), (7, 2, 1), (12, 0, 3), (12, 0, 0), (8, 2, 1), (6, 2, 3), (7, 2, 3), (9, 2, 1), (10, 2, 2), (10, 2, 0), (12, 1, 2), (8, 2, 3), (9, 2, 3), (12, 1, 0), (10, 2, 1), (12, 1, 3), (11, 2, 2), (12, 0, 2), (11, 2, 0), (10, 2, 3), (11, 2, 1), (12, 0, 1), (12, 2, 2), (12, 2, 0), (12, 2, 1), (11, 2, 3), (12, 2, 3))


def kernel(names, src, cnt, feats, w_hbm, out_ref, *scratch):
    ref = dict(zip(names, scratch))
    w, table, scale = ref["w"], ref["table"], ref["scale"]
    row, col = lax.axis_index("row"), lax.axis_index("col")
    core, zh, y = row % 2, (row // 2) % 2, row // 4
    x, zl = col % 4, col // 4
    other_core = (row + 1 - 2 * core, col)
    y_next = (((y + 1) % 4) * 4 + row % 4, col)
    y_far = (((y + 2) % 4) * 4 + row % 4, col)
    y_prev = (((y + 3) % 4) * 4 + row % 4, col)
    z_far = (row + 2 - 4 * zh, col)
    z_near = (row, col + 4 - 8 * zl)
    x_next = (row, zl * 4 + (x + 1) % 4)
    x_far = (row, zl * 4 + (x + 2) % 4)
    x_prev = (row, zl * 4 + (x + 3) % 4)
    sends = {(k, ch): [] for k in range(ITERS) for ch in range(CHUNKS)}

    def remote(kind, tag, index, source, target, device, keep=True, begin=True):
        copy = pltpu.make_async_remote_copy(
            src_ref=source,
            dst_ref=target,
            send_sem=ref["s_" + kind, tag].at[index],
            recv_sem=ref["r_" + kind, tag].at[index],
            device_id=device,
            device_id_type=MESH,
        )
        if begin:
            copy.start()
        if keep:
            sends[tag].append(copy)

    def arrived(kind, tag, index, target):
        pltpu.make_async_remote_copy(
            src_ref=target,
            dst_ref=target,
            send_sem=ref["s_" + kind, tag].at[index],
            recv_sem=ref["r_" + kind, tag].at[index],
            device_id=other_core,
            device_id_type=MESH,
        ).wait_recv()

    barrier = pltpu.get_barrier_semaphore()
    peers = (other_core, y_next, y_prev, y_far, z_far, z_near, x_next, x_prev, x_far)
    for peer in peers:
        pl.semaphore_signal(barrier, inc=1, device_id=peer, device_id_type=MESH)
    w_copy = pltpu.make_async_copy(w_hbm, w, ref["w_sem"].at[0])
    loads = []
    for g in range(4):
        ch, part = g // (4 // CHUNKS), g % (4 // CHUNKS)
        first = pl.multiple_of(col * GROUP + part * 8, 8)
        target = ref["x", (0, ch)].at[pl.ds(0, SRCS), pl.ds(first, 8), :]
        loads.append(pltpu.make_async_copy(feats.at[g], target, ref["x_sem"].at[g]))
        loads[-1].start()
    w_copy.start()
    for k in range(ITERS):
        for ch in range(CHUNKS):
            xs = ref["x", (k, ch)]
            xs[SRCS] = jnp.zeros((rows_of(k, ch), TILE), BF16)
    first_row = lax.broadcasted_iota(jnp.int32, (SRCS, TAIL, TILE), 1) == 0
    ref["x", (0, 0)][0:SRCS, WIDE : WIDE + TAIL, :] = jnp.where(first_row, 1.0, 0.0).astype(BF16)

    def build_table():
        def one(q, start):
            count = cnt[0, q]
            for j in range(MOST):
                slot = jnp.minimum(start + j, SLOTS - 1)
                table[q * MOST + j] = jnp.where(j < count, src[0, slot], SRCS)
            table[DESTS * MOST + q] = start
            return start + count

        lax.fori_loop(0, DESTS, one, jnp.int32(0))

    build_table()
    pl.semaphore_wait(barrier, len(peers))

    def block(k, ch, who, half=None):
        xs = ref["x", (k, ch)]
        if k == 0:
            feat = pl.ds(pl.multiple_of(who * GROUP, GROUP), GROUP)
            if half is None:
                return xs.at[pl.ds(0, SRCS), feat, :]
            return xs.at[pl.ds(half * (SRCS // 2), SRCS // 2), feat, :]
        if half is None:
            return xs.at[pl.ds(who * 4, 4)]
        return xs.at[pl.ds(who * 4 + half * 2, 2)]

    z_col = col + 4 - 8 * zl
    next_col, prev_col = zl * 4 + (x + 1) % 4, zl * 4 + (x + 3) % 4
    far_col = zl * 4 + (x + 2) % 4
    z_next, z_prev = next_col + 4 - 8 * zl, prev_col + 4 - 8 * zl
    z_across = far_col + 4 - 8 * zl

    def gather_0(k, ch):
        mine = block(k, ch, col)
        source = mine if k else feats.at[ch]
        remote("ag", (k, ch), 0, source, mine, z_near)
        if k:
            remote("ag", (k, ch), 3, source, mine, x_far)
        remote("ag", (k, ch), 1, source, mine, x_next)
        remote("ag", (k, ch), 2, source, mine, x_prev)

    def gather_1(k, ch):
        theirs = block(k, ch, z_col)
        arrived("ag", (k, ch), 0, theirs)
        if k:
            remote("ag", (k, ch), 6, theirs, theirs, x_far)
            remote("ag", (k, ch), 4, theirs, theirs, x_next)
            remote("ag", (k, ch), 5, theirs, theirs, x_prev)
        else:
            remote("ag", (k, ch), 3, theirs, theirs, x_next)
            remote("ag", (k, ch), 4, theirs, theirs, x_prev)

    def pass_p(k, ch, base, who):
        arrived("ag", (k, ch), base, block(k, ch, who))
        half = block(k, ch, who, 0)
        remote("ag", (k, ch), base + 4, half, half, x_next)

    def pass_m(k, ch, base, who):
        arrived("ag", (k, ch), base + 1, block(k, ch, who))
        half = block(k, ch, who, 1)
        remote("ag", (k, ch), base + 5, half, half, x_prev)

    def gather_2(k, ch):
        pass_p(k, ch, 1, prev_col)
        pass_m(k, ch, 1, next_col)

    def gather_3(k, ch):
        pass_p(k, ch, 3, z_prev)
        pass_m(k, ch, 3, z_next)

    def gather_4(k, ch):
        if k:
            who = (prev_col, next_col, far_col, z_prev, z_next, z_across)
            for i in range(6):
                arrived("ag", (k, ch), i + 1, block(k, ch, who[i]))
        else:
            arrived("ag", (k, ch), 5, block(k, ch, far_col, 0))
            arrived("ag", (k, ch), 6, block(k, ch, far_col, 1))
            arrived("ag", (k, ch), 7, block(k, ch, z_across, 0))
            arrived("ag", (k, ch), 8, block(k, ch, z_across, 1))

    def products(k, ch, q):
        xs = ref["x", (k, ch)]
        start = table[DESTS * MOST + q]
        left = jnp.concatenate([xs[table[q * MOST + j]] for j in range(MOST)], axis=1)
        right = jnp.concatenate(
            [w[jnp.minimum(start + j, SLOTS - 1)] for j in range(MOST)], axis=0
        )
        return jnp.dot(left, right, preferred_element_type=F32)

    def tail_sum(terms):
        total = None
        for term in terms:
            part = jnp.sum(term[WIDE:, :].astype(F32), axis=0, keepdims=True)
            total = part if total is None else total + part
        return total

    def add_up(terms):
        total = terms[0][:WIDE, :].astype(F32)
        for term in terms[1:]:
            total = total + term[:WIDE, :].astype(F32)
        return total

    def put(target, terms):
        target[0:WIDE, :] = add_up(terms).astype(BF16)
        if terms[0].shape[0] > WIDE:
            total = tail_sum(terms)
            high = total.astype(BF16).astype(F32)
            low = total - high
            which = lax.broadcasted_iota(jnp.int32, (TAIL, TILE), 0)
            split = jnp.where(which == 0, high, jnp.where(which == 1, low, 0.0))
            target[WIDE : WIDE + TAIL, :] = split.astype(BF16)

    def first_dest(i, side):
        zi, yi = i // 4, i % 4
        hop = (2 + 3 * yi + 3 * ((yi * (yi - 1)) // 2)) % 4
        z = (1 - zh + zi) % 2
        return (((y + hop) % 4) * 4 + z * 2 + side) * 4

    def core_copy(k, ch, pair, **how):
        give, take = ref["give", (k, ch)], ref["take", (k, ch)]
        both = pl.ds(pair * 2, 2)
        remote("core", (k, ch), pair, give.at[both], take.at[both], other_core, **how)

    def make_given(k, ch):
        give = ref["give", (k, ch)]

        def one(pair, carry):
            sums = [products(k, ch, first_dest(pair * 2 + e, 1 - core) + t) for e in range(2) for t in range(4)]
            for e in range(2):
                for t in range(4):
                    put(give.at[pair * 2 + e, t], [sums[e * 4 + t]])
            core_copy(k, ch, pair, keep=False)
            return carry

        lax.fori_loop(0, 4, one, 0)
        for pair in range(4):
            core_copy(k, ch, pair, begin=False)

    def y_first(k, ch, zi, **how):
        tag, own = (k, ch), ref["own", (k, ch)]
        remote("y", tag, zi * 3, own.at[zi * 4], ref["far", tag].at[zi], y_far, **how)
        remote("y", tag, zi * 3 + 1, own.at[zi * 4 + 1], ref["near_p", tag].at[zi], y_next, **how)

    def y_second(k, ch, zi, **how):
        tag, own = (k, ch), ref["own", (k, ch)]
        remote("y", tag, zi * 3 + 2, own.at[zi * 4 + 2], ref["near_m", tag].at[zi], y_prev, **how)

    def make_own(k, ch, zi):
        own, take = ref["own", (k, ch)], ref["take", (k, ch)]

        def one(h, carry):
            pair = zi * 2 + h
            sums = [products(k, ch, first_dest(pair * 2 + e, core) + t) for e in range(2) for t in range(4)]
            arrived("core", (k, ch), pair, take.at[pl.ds(pair * 2, 2)])
            for e in range(2):
                i = pair * 2 + e
                for t in range(4):
                    put(own.at[i, t], [sums[e * 4 + t], take[i, t]])

            @pl.when(h == 0)
            def _():
                y_first(k, ch, zi, keep=False)

            @pl.when(h == 1)
            def _():
                y_second(k, ch, zi, keep=False)

            return carry

        lax.fori_loop(0, 2, one, 0)
        y_first(k, ch, zi, begin=False)
        y_second(k, ch, zi, begin=False)

    def own_0(k, ch):
        make_own(k, ch, 0)

    def own_1(k, ch):
        make_own(k, ch, 1)

    def y_terms(k, ch, zi):
        buffers = [ref[name, (k, ch)] for name in ("far", "near_p", "near_m")]
        for i, buffer in enumerate(buffers):
            arrived("y", (k, ch), zi * 3 + i, buffer.at[zi])
        own = ref["own", (k, ch)]
        return [[own[zi * 4 + 3, t]] + [buffer[zi, t] for buffer in buffers] for t in range(4)]

    def z_send(k, ch):
        tag = (k, ch)
        z_out = ref["z_out", tag]
        terms = y_terms(k, ch, 0)
        for t in range(4):
            put(z_out.at[t], terms[t])
        remote("z", tag, 0, z_out, ref["z_in", tag], z_far)

    def finish(k, ch):
        tag = (k, ch)
        z_in = ref["z_in", tag]
        sums = y_terms(k, ch, 1)
        arrived("z", tag, 0, z_in)
        for t in range(4):
            terms = sums[t] + [z_in[t]]
            if tag == (0, 0):
                scale[t] = (1.0 - TELEPORT) / (1.0 + tail_sum(terms))
            here = col * 4 + t
            old = ref["x", tag][here, 0:WIDE, :].astype(F32)
            start = ref["x", (0, ch)][here, 0:WIDE, :].astype(F32)
            new = ((add_up(terms) + old) * scale[t] + TELEPORT * start).astype(BF16)
            if k + 1 < ITERS:
                ref["x", (k + 1, ch)][here, 0:WIDE, :] = new
            else:
                for g in range(8):
                    low = g * 32 + ch * GROUP
                    out_ref[t, low : low + GROUP, :] = new[g * GROUP : (g + 1) * GROUP, :]

    def drain(k, ch):
        for copy in sends[k, ch]:
            copy.wait_send()

    def load(k, ch):
        loads[ch].wait()

    def weights(k, ch):
        w_copy.wait()

    tasks = dict(
        load=load,
        weights=weights,
        gather_0=gather_0,
        gather_1=gather_1,
        gather_2=gather_2,
        gather_3=gather_3,
        gather_4=gather_4,
        give=make_given,
        own_0=own_0,
        own_1=own_1,
        z_send=z_send,
        finish=finish,
        drain=drain,
    )
    for number, k, ch in ORDER:
        tasks[NAMES[number]](k, ch)

def on_device(features, tile_vals, tile_src, row_counts):
    feats = features.T.reshape(4, 8, SRCS, TILE).transpose(0, 2, 1, 3)
    shapes = scratch_layout()
    out = pl.pallas_call(
        functools.partial(kernel, tuple(shapes)),
        out_shape=jax.ShapeDtypeStruct((4, FEATS, TILE), BF16),
        in_specs=[pl.BlockSpec(memory_space=pltpu.SMEM)] * 2
        + [pl.BlockSpec(memory_space=pl.ANY)] * 2,
        out_specs=pl.BlockSpec(memory_space=pltpu.VMEM),
        scratch_shapes=list(shapes.values()),
        compiler_params=pltpu.CompilerParams(
            collective_id=0, has_side_effects=True, vmem_limit_bytes=58 * 2**20
        ),
        name="propagate",
    )(tile_src, row_counts, feats, tile_vals)
    return out.transpose(0, 2, 1).reshape(4 * TILE, FEATS)


def solution(mesh):
    placed = (P("row", "col"), P("row", "col", None), P("row", "col"), P("row", "col"))
    return jax.shard_map(
        on_device, mesh=mesh, in_specs=placed, out_specs=P(("row", "col"), None), check_vma=False
    )
```

time: 123 us -> 108 us (0.88)
  Pallas kernels: 122 us -> 106 us
    pallas_call x1, Pallas kernels: 122 us -> 106 us  [on_device(): pl.pallas_call(functools.partial(kernel, tuple(shapes)), out_shape=jax.Sh...]
where the time goes in v3:
time: 108 us
  Pallas kernels  106 us (98%)
  local copies, waits for them, and re-layouts  1.79 us (2%)
    pallas_call x1, Pallas kernels, on_device(): pl.pallas_call(functools.partial(kernel, tuple(shapes)), out_shape=jax.Sh...  106 us

profile of v3, /device:TPU:0, one launch (start us, length us, event | category | flops | bytes accessed | tf_op | source)
XLA Modules:
  0.0 107.6 jit_solution(11848206364934451970)
XLA Ops:
  0.0 105.8 %propagate.1 = bf16[4,256,128]{2,1,0:T(8,128)(2,1)} custom-call(s32[1,256]{1,0:T(1,128)} %src.1, s32[1,64]{1,0:T(1,128)} %cnt.1, bf16[4,32,8,128]{3,2,1,0:T(8,128)(2,1)} %bitcast.8, bf16[256,128,128]{2,1,0:T(8,128)(2,1)} %w_hbm.1), custom_call_target="tpu_custom_call" | custom-call | tf_op jit(solution)/shard_map/propagate/pallas_call | solution.py:379
  105.8 1.8 %copy.5 = bf16[4,128,256]{2,1,0:T(8,128)(2,1)} copy(bf16[4,128,256]{1,2,0:T(8,128)(2,1)} %bitcast.7) | data formatting | bytes 524288 | tf_op jit(solution)/shard_map/transpose | solution.py:391

commit v4 on v3

--- a/solution.py
+++ b/solution.py
@@ -67,7 +67,7 @@
     "finish",
     "drain",
 )
-ORDER = ((2, 0, 0), (2, 0, 1), (2, 0, 2), (3, 0, 0), (4, 0, 0), (3, 0, 2), (0, 0, 2), (1, 0, 0), (5, 0, 0), (4, 0, 2), (4, 0, 1), (5, 0, 2), (3, 0, 1), (2, 0, 3), (0, 0, 0), (6, 0, 0), (7, 0, 0), (6, 0, 2), (7, 0, 2), (8, 0, 0), (3, 0, 3), (9, 0, 0), (8, 0, 2), (9, 0, 2), (4, 0, 3), (5, 0, 1), (10, 0, 0), (5, 0, 3), (0, 0, 1), (0, 0, 3), (6, 0, 1), (7, 0, 1), (6, 0, 3), (11, 0, 0), (2, 1, 0), (10, 0, 2), (8, 0, 1), (7, 0, 3), (3, 1, 0), (9, 0, 1), (11, 0, 2), (2, 1, 2), (10, 0, 1), (8, 0, 3), (9, 0, 3), (6, 1, 0), (3, 1, 2), (7, 1, 0), (11, 0, 1), (2, 1, 1), (10, 0, 3), (8, 1, 0), (9, 1, 0), (6, 1, 2), (3, 1, 1), (7, 1, 2), (11, 0, 3), (2, 1, 3), (10, 1, 0), (8, 1, 2), (6, 1, 1), (7, 1, 1), (3, 1, 3), (9, 1, 2), (11, 1, 0), (2, 2, 0), (10, 1, 2), (8, 1, 1), (9, 1, 1), (6, 1, 3), (3, 2, 0), (7, 1, 3), (11, 1, 2), (10, 1, 1), (2, 2, 2), (8, 1, 3), (6, 2, 0), (7, 2, 0), (3, 2, 2), (11, 1, 1), (2, 2, 1), (9, 1, 3), (10, 1, 3), (8, 2, 0), (9, 2, 0), (3, 2, 1), (6, 2, 2), (7, 2, 2), (11, 1, 3), (2, 2, 3), (12, 1, 1), (8, 2, 2), (9, 2, 2), (6, 2, 1), (3, 2, 3), (7, 2, 1), (12, 0, 3), (12, 0, 0), (8, 2, 1), (6, 2, 3), (7, 2, 3), (9, 2, 1), (10, 2, 2), (10, 2, 0), (12, 1, 2), (8, 2, 3), (9, 2, 3), (12, 1, 0), (10, 2, 1), (12, 1, 3), (11, 2, 2), (12, 0, 2), (11, 2, 0), (10, 2, 3), (11, 2, 1), (12, 0, 1), (12, 2, 2), (12, 2, 0), (12, 2, 1), (11, 2, 3), (12, 2, 3))
+ORDER = ((2, 0, 0), (2, 0, 2), (2, 0, 1), (4, 0, 0), (3, 0, 0), (3, 0, 1), (3, 0, 2), (5, 0, 0), (4, 0, 1), (0, 0, 1), (0, 0, 0), (5, 0, 1), (2, 0, 3), (5, 0, 2), (0, 0, 2), (1, 0, 0), (4, 0, 2), (6, 0, 0), (7, 0, 0), (6, 0, 1), (7, 0, 1), (8, 0, 0), (9, 0, 0), (3, 0, 3), (4, 0, 3), (0, 0, 3), (6, 0, 2), (7, 0, 2), (8, 0, 1), (10, 0, 0), (9, 0, 1), (5, 0, 3), (6, 0, 3), (11, 0, 0), (2, 1, 0), (10, 0, 1), (8, 0, 2), (7, 0, 3), (3, 1, 0), (9, 0, 2), (11, 0, 1), (2, 1, 1), (10, 0, 2), (8, 0, 3), (9, 0, 3), (6, 1, 0), (3, 1, 1), (7, 1, 0), (11, 0, 2), (2, 1, 2), (10, 0, 3), (8, 1, 0), (9, 1, 0), (6, 1, 1), (3, 1, 2), (7, 1, 1), (11, 0, 3), (2, 1, 3), (10, 1, 0), (8, 1, 1), (6, 1, 2), (7, 1, 2), (3, 1, 3), (9, 1, 1), (11, 1, 0), (2, 2, 0), (12, 1, 0), (10, 1, 1), (8, 1, 2), (9, 1, 2), (6, 1, 3), (3, 2, 0), (7, 1, 3), (11, 1, 1), (2, 2, 1), (10, 1, 2), (8, 1, 3), (9, 1, 3), (6, 2, 0), (3, 2, 1), (7, 2, 0), (11, 1, 2), (2, 2, 2), (12, 1, 2), (10, 1, 3), (8, 2, 0), (6, 2, 1), (9, 2, 0), (3, 2, 2), (7, 2, 1), (11, 1, 3), (2, 2, 3), (8, 2, 1), (6, 2, 2), (7, 2, 2), (3, 2, 3), (9, 2, 1), (12, 0, 3), (8, 2, 2), (10, 2, 1), (9, 2, 2), (10, 2, 0), (6, 2, 3), (7, 2, 3), (12, 0, 1), (8, 2, 3), (11, 2, 1), (11, 2, 0), (12, 0, 0), (10, 2, 2), (12, 1, 3), (9, 2, 3), (10, 2, 3), (12, 2, 0), (12, 2, 1), (12, 0, 2), (11, 2, 2), (12, 1, 1), (12, 2, 2), (11, 2, 3), (12, 2, 3))
 
 
 def kernel(names, src, cnt, feats, w_hbm, out_ref, *scratch):
@@ -257,15 +257,16 @@
     def make_given(k, ch):
         give = ref["give", (k, ch)]
 
-        def one(pair, carry):
-            sums = [products(k, ch, first_dest(pair * 2 + e, 1 - core) + t) for e in range(2) for t in range(4)]
-            for e in range(2):
+        def one(half, carry):
+            sums = [products(k, ch, first_dest(half * 4 + e, 1 - core) + t) for e in range(4) for t in range(4)]
+            for e in range(4):
                 for t in range(4):
-                    put(give.at[pair * 2 + e, t], [sums[e * 4 + t]])
-            core_copy(k, ch, pair, keep=False)
+                    put(give.at[half * 4 + e, t], [sums[e * 4 + t]])
+            for p in range(2):
+                core_copy(k, ch, half * 2 + p, keep=False)
             return carry
 
-        lax.fori_loop(0, 4, one, 0)
+        lax.fori_loop(0, 2, one, 0)
         for pair in range(4):
             core_copy(k, ch, pair, begin=False)
 

time: 108 us -> 109 us (level)
  Pallas kernels: 106 us -> 108 us
    pallas_call x1, Pallas kernels: 106 us -> 108 us  [on_device(): pl.pallas_call(functools.partial(kernel, tuple(shapes)), out_shape=jax.Sh...]
where the time goes in v4:
time: 109 us
  Pallas kernels  108 us (99%)
  local copies, waits for them, and re-layouts  1.79 us (2%)
    pallas_call x1, Pallas kernels, on_device(): pl.pallas_call(functools.partial(kernel, tuple(shapes)), out_shape=jax.Sh...  108 us

profile of v4, /device:TPU:0, one launch (start us, length us, event | category | flops | bytes accessed | tf_op | source)
XLA Modules:
  0.0 109.4 jit_solution(6297012092784774671)
XLA Ops:
  0.0 107.6 %propagate.1 = bf16[4,256,128]{2,1,0:T(8,128)(2,1)} custom-call(s32[1,256]{1,0:T(1,128)} %src.1, s32[1,64]{1,0:T(1,128)} %cnt.1, bf16[4,32,8,128]{3,2,1,0:T(8,128)(2,1)} %bitcast.8, bf16[256,128,128]{2,1,0:T(8,128)(2,1)} %w_hbm.1), custom_call_target="tpu_custom_call" | custom-call | tf_op jit(solution)/shard_map/propagate/pallas_call | solution.py:380
  107.6 1.8 %copy.5 = bf16[4,128,256]{2,1,0:T(8,128)(2,1)} copy(bf16[4,128,256]{1,2,0:T(8,128)(2,1)} %bitcast.7) | data formatting | bytes 524288 | tf_op jit(solution)/shard_map/transpose | solution.py:392
